TPU v7x, 32 devices: a whole 2x2x4 slice. The times are simulated.
32 devices in a mesh: clip: 16 (over z, y, x), row: 2 (over core).
Axes of the slice: x: 2, y: 2, z: 4, core: 2. Of those that a mesh axis runs over, the one named last changes fastest.
Arguments:
- queries: bfloat16 [16, 512, 1792], P('clip', 'row'), may hold values from -36 to 36
- frames_kv: bfloat16 [16, 512, 512], P('clip', 'row'), may hold values from -20 to 20
- summary_kv: bfloat16 [16, 32, 512], P('clip', 'row'), may hold values from -6 to 6
- lengths: int32 [16], P('clip'), may hold values from 128 to 512, as said below
- caps: int32 [16], P('clip'), may hold values from 8 to 32, as said below
Outputs:
- attended: bfloat16 [16, 512, 1792], P('clip', 'row')
Inputs may be any that keep to these rules, and one draw needn't show every extreme that they name: `lengths`: some clip of every draw has 512 frame tokens. `caps`: some clip of every draw keeps 32 summary tokens.
All inputs are finite; a program needn't handle non-finite values.
Results may differ from a plain program's by a relative error of at most 0.01.
Values may be sent and summed in bfloat16 or wider, within the bound.
A program may use at most 64 MiB of HBM per device.

v0:
```python
import math
import jax
import jax.numpy as jnp
from jax import lax
from jax.sharding import PartitionSpec as P

KVH = 2
HD = 128
WINDOW = 128
masked_score = -1e30


def passed_along(block, axis, distance):
    devices = range(lax.axis_size(axis))
    route = [(i - distance, i) for i in devices if i - distance in devices]
    return lax.ppermute(block, axis, route)


def attend(state, query_heads, keys, values, valid):
    largest, total, accum = state
    scores = jnp.einsum(
        "tkgd,skd->kgts", query_heads, keys, preferred_element_type=jnp.float32
    ) * HD ** (-0.5)
    masked = jnp.where(valid, scores, masked_score)
    fresh = jnp.maximum(largest, jnp.max(masked, axis=-1))
    weights = jnp.where(valid, jnp.exp(masked - fresh[..., None]), 0.0)
    factor = jnp.exp(largest - fresh)
    total = total * factor + jnp.sum(weights, axis=-1)
    accum = accum * factor[..., None] + jnp.einsum(
        "kgts,skd->kgtd", weights.astype(jnp.bfloat16), values, preferred_element_type=jnp.float32
    )
    return (fresh, total, accum)


def split_rows(kv_rows):
    count = kv_rows.shape[0]
    keys = kv_rows[:, : KVH * HD].reshape(count, KVH, HD)
    values = kv_rows[:, KVH * HD :].reshape(count, KVH, HD)
    return (keys, values)


def fold_summary(state, piece, query_heads, clip_index):
    rows_kv, clip_caps = piece
    clip_count = rows_kv.shape[0]
    slot_count = rows_kv.shape[1]
    flat = rows_kv.reshape(clip_count * slot_count, rows_kv.shape[2])
    clip_ids = jnp.arange(clip_count)
    live = (jnp.arange(slot_count)[None, :] < clip_caps[:, None]) & (clip_ids[:, None] < clip_index)
    live = live.reshape(-1)
    count = clip_count * slot_count
    block = math.gcd(count, 512)
    blocks_kv = flat.reshape(count // block, block, flat.shape[1])
    blocks_live = live.reshape(count // block, block)

    def step_block(carry, item):
        kv_block, live_block = item
        keys, values = split_rows(kv_block)
        return (attend(carry, query_heads, keys, values, live_block), None)

    state, unused = lax.scan(step_block, state, (blocks_kv, blocks_live))
    return state


def shards(queries, frames_kv, summary_kv, lengths, caps):
    tokens_here = queries.shape[1]
    group = queries.shape[2] // (KVH * HD)
    row_index = lax.axis_index("row")
    clip_index = lax.axis_index("clip")
    own_heads = queries[0].reshape(tokens_here, KVH, group, HD)
    frames = frames_kv[0]
    rim = passed_along(frames[tokens_here - WINDOW :], "row", 1)
    local_kv = jnp.concatenate([rim, frames], axis=0)
    query_pos = row_index * tokens_here + jnp.arange(tokens_here)
    key_pos = row_index * tokens_here - WINDOW + jnp.arange(WINDOW + tokens_here)
    near = (
        (key_pos[None, :] >= 0)
        & (key_pos[None, :] <= query_pos[:, None])
        & (key_pos[None, :] > query_pos[:, None] - WINDOW)
    )
    start_state = (
        jnp.full((KVH, group, tokens_here), masked_score, jnp.float32),
        jnp.zeros((KVH, group, tokens_here), jnp.float32),
        jnp.zeros((KVH, group, tokens_here, HD), jnp.float32),
    )
    local_keys, local_values = split_rows(local_kv)
    state = attend(start_state, own_heads, local_keys, local_values, near)
    collected, every_cap = (
        lax.all_gather(summary_kv, "clip", axis=0, tiled=True),
        lax.all_gather(caps, "clip", axis=0, tiled=True),
    )
    state = fold_summary(
        state,
        (lax.all_gather(collected, "row", axis=1, tiled=True), every_cap),
        own_heads,
        clip_index,
    )
    largest, total, accum = state
    result = accum / total[..., None]
    result = jnp.transpose(result, (2, 0, 1, 3)).reshape(tokens_here, KVH * group * HD)
    result = jnp.where((query_pos < lengths[0])[:, None], result, 0.0)
    return result.astype(jnp.bfloat16)[None]


def solution(mesh):
    placed = (
        P("clip", "row", None),
        P("clip", "row", None),
        P("clip", "row", None),
        P("clip"),
        P("clip"),
    )
    return jax.shard_map(
        shards, mesh=mesh, in_specs=placed, out_specs=P("clip", "row", None), check_vma=False
    )
```

profile of v0, /device:TPU:28, one launch (start us, length us, event | category | flops | bytes accessed | tf_op | source)
XLA Modules:
  0.0 79.2 jit_solution(14224585013635414499)
XLA Ops:
  0.0 1.1 %copy.36 = bf16[1,256,512]{1,2,0:T(8,128)(2,1)S(1)} copy(bf16[1,256,512]{2,1,0:T(8,128)(2,1)} %param.6) | data formatting | bytes 524288 | tf_op args[1]
  1.1 1.7 %collective-permute-start = (bf16[128,512]{0,1:T(8,128)(2,1)S(1)}, bf16[128,512]{0,1:T(8,128)(2,1)S(1)}, u32[]{:S(2)}, u32[]{:S(2)}) collective-permute-start(bf16[128,512]{0,1:T(8,128)(2,1)S(1)} %slice_bitcast_fusion), channel_id=1, source_target_pairs={{0,1},{2,3},{4,5},{6,7},{8,9},{10,11},{12,13},{14,15},{16,17},{18,... | collective-permute-start | bytes 393224 | tf_op jit(solution)/shard_map/ppermute | solution.py:16
  2.9 36.1 %all_gather.10 = bf16[16,16,512]{2,1,0:T(8,128)(2,1)S(1)} all-gather(bf16[1,16,512]{2,1,0:T(8,128)(2,1)} %param.7), channel_id=1, replica_groups=mesh['clip'=16,'row'=2] {'clip'}, dimensions={0}, use_global_device_ids=true | all-gather | bytes 278528 | tf_op jit(solution)/shard_map/all_gather | solution.py:88
  39.0 2.2 %all_gather.11 = bf16[16,32,512]{2,1,0:T(8,128)(2,1)S(1)} all-gather(bf16[16,16,512]{2,1,0:T(8,128)(2,1)S(1)} %all_gather.10), channel_id=1, replica_groups=mesh['clip'=16,'row'=2] {'row'}, dimensions={1}, use_global_device_ids=true | all-gather | bytes 786432 | tf_op jit(solution)/shard_map/all_gather | solution.py:93
  41.8 1.2 %dynamic-slice = u32[1]{0:T(128)} dynamic-slice(u32[32]{0:T(128)} %constant.52, u32[]{:T(128)S(6)} %add.72), dynamic_slice_sizes={1} | dynamic-slice | bytes 12
  43.1 0.8 dynamic-update-slice
  43.8 16.8 %all-reduce = s32[16]{0:T(128)S(1)} all-reduce(s32[16]{0:T(128)S(1)} %dynamic-update-slice), channel_id=1, replica_groups=mesh['clip'=16,'row'=2] {'clip'}, use_global_device_ids=true, to_apply=%add | all-reduce | flops 16 | bytes 128
  60.7 0.1 fusion.23
  60.8 0.1 and.30
  60.8 0.1 copy.42
  61.0 1.5 %copy.38 = bf16[1,256,1792]{1,2,0:T(8,128)(2,1)S(1)} copy(bf16[1,256,1792]{2,1,0:T(8,128)(2,1)} %param.5) | data formatting | bytes 1835008 | tf_op args[0]
  62.5 4.3 %bitcast_reduce_fusion = (f32[2,7,256]{2,1,0:T(8,128)S(1)}, f32[2,512,256,7]{2,1,3,0:T(8,128)}) fusion(pred[512]{0:T(512)(128)(4,1)S(1)} %and.30, bf16[512,2,128,1]{0,2,3,1:T(8,128)(2,1)S(1)} %bitcast.95, bf16[256,2,7,128]{0,3,2,1:T(8,128)(2,1)S(1)} %bitcast.91), kind=kOutput, calls=%fused_computation.1 | convolution fusion | flops 475263488 | bytes 8534528 | tf_op jit(solution)/shard_map/while/body/eval_jaxpr/tkgd,skd->kgts/dot_general | solution.py:21
  66.7 0.2 compare_and_fusion
  66.9 0.1 copy.45
  67.0 0.0 copy-start
  67.9 0.0 collective-permute-done
  67.9 0.1 pad_maximum_fusion
  67.9 1.1 %fusion.4 = (f32[2,7,256]{2,1,0:T(8,128)S(1)}, f32[2,384,256,7]{2,1,3,0:T(8,128)S(1)}) fusion(pred[256,384]{0,1:T(8,128)(4,1)S(1)} %compare_and_fusion, bf16[384,2,128,1]{0,2,3,1:T(8,128)(2,1)S(1)} %bitcast.97, bf16[256,2,7,128]{0,3,2,1:T(8,128)(2,1)S(1)} %bitcast.92), kind=kOutput, calls=%fused_computation.9 | convolution fusion | flops 356446720 | bytes 6731776 | tf_op jit(solution)/shard_map/tkgd,skd->kgts/dot_general | solution.py:21
  69.0 1.1 %copy-done = f32[2,512,256,7]{2,1,3,0:T(8,128)S(1)} copy-done((f32[2,512,256,7]{2,1,3,0:T(8,128)S(1)}, f32[2,512,256,7]{2,1,3,0:T(8,128)}, u32[]{:S(2)}) %copy-start) | copy-done | bytes 7340056
  70.1 2.1 %fusion.2 = f32[2,7,256]{2,1,0:T(8,128)S(1)} fusion(f32[2,512,256,7]{2,1,3,0:T(8,128)S(1)} %copy-done, f32[2,7,256]{2,1,0:T(8,128)S(1)} %get-tuple-element.34, pred[512]{0:T(512)(128)(4,1)S(1)} %and.30), kind=kLoop, calls=%fused_computation.7 | loop fusion | flops 9171456 | bytes 7369216 | tf_op jit(solution)/shard_map/while/body/eval_jaxpr/reduce_sum | solution.py:28
  72.2 2.0 %fusion.7 = f32[2,7,256,128]{2,3,1,0:T(8,128)S(1)} fusion(bf16[512,2,128,1]{0,2,3,1:T(8,128)(2,1)S(1)} %bitcast.98, f32[2,512,256,7]{2,1,3,0:T(8,128)S(1)} %copy-done, f32[2,7,256]{2,1,0:T(8,128)S(1)} %get-tuple-element.34, pred[512]{0:T(512)(128)(4,1)S(1)} %and.30), kind=kOutput, calls=%fused_computation.12 | convolution fusion | flops 478937088 | bytes 9452032 | tf_op jit(solution)/shard_map/while/body/eval_jaxpr/kgts,skd->kgtd/dot_general | solution.py:29
  74.2 1.3 %fusion.5 = f32[2,7,256]{2,1,0:T(8,128)S(1)} fusion(f32[2,384,256,7]{2,1,3,0:T(8,128)S(1)} %get-tuple-element.36, f32[2,7,256]{2,1,0:T(8,128)S(1)} %get-tuple-element.33, pred[256,384]{0,1:T(8,128)(4,1)S(1)} %compare_and_fusion), kind=kLoop, calls=%fused_computation.10 | loop fusion | flops 6877696 | bytes 5632000 | tf_op jit(solution)/shard_map/reduce_sum | solution.py:28
  75.6 1.9 %fusion.14 = bf16[256,2,7,128]{0,3,2,1:T(8,128)(2,1)S(1)} fusion(f32[2,7,256,128]{2,3,1,0:T(8,128)S(1)} %fusion.7, bf16[384,2,128,1]{0,2,3,1:T(8,128)(2,1)S(1)} %bitcast.99, f32[2,384,256,7]{2,1,3,0:T(8,128)S(1)} %get-tuple-element.36, f32[2,7,256]{2,1,0:T(8,128)S(1)} %get-tuple-element.33, pred[256,384]{0,1:T(8,128)(4,1)S(1)} %compare_and_fusion, ...), kind=kOutput, calls=%fused_computation.18 | convolution fusion | flops 361496576 | bytes 8609792 | tf_op jit(solution)/shard_map/kgts,skd->kgtd/dot_general | solution.py:29
  77.5 0.6 copy.47
  78.1 1.1 %select_convert_fusion = bf16[1,256,1792]{2,1,0:T(8,128)(2,1)} fusion(bf16[1,256,1792]{2,1,0:T(8,128)(2,1)S(1)} %copy.47, pred[256]{0:T(512)(128)(4,1)S(1)} %fusion.25), kind=kLoop, calls=%fused_computation.21 | loop fusion | flops 458752 | bytes 1835264 | tf_op jit(solution)/shard_map/convert_element_type | solution.py:101
  (10 shorter events, 0.1 us)
Async XLA Ops:
  1.1 66.8 %collective-permute-start = (bf16[128,512]{0,1:T(8,128)(2,1)S(1)}, bf16[128,512]{0,1:T(8,128)(2,1)S(1)}, u32[]{:S(2)}, u32[]{:S(2)}) collective-permute-start(bf16[128,512]{0,1:T(8,128)(2,1)S(1)} %slice_bitcast_fusion), channel_id=1, source_target_pairs={{0,1},{2,3},{4,5},{6,7},{8,9},{10,11},{12,13},{14,15},{16,17},{18,... | collective-permute-start | bytes 393224 | tf_op jit(solution)/shard_map/ppermute | solution.py:16
  67.0 3.1 %copy-start = (f32[2,512,256,7]{2,1,3,0:T(8,128)S(1)}, f32[2,512,256,7]{2,1,3,0:T(8,128)}, u32[]{:S(2)}) copy-start(f32[2,512,256,7]{2,1,3,0:T(8,128)} %get-tuple-element.38) | copy-start | bytes 22020100
where the time goes:
time: 79.5 us; the launch traced here: 79.2 us
  blocking collectives  55.1 us (69%)
  matrix products  9.2 us (12%)
  local copies, waits for them, and re-layouts  6.69 us (8%)
  other arithmetic  4.89 us (6%)
  starting transfers between devices  1.75 us (2%)
  between operations  1.64 us (2%)
    all_gather x1, blocking collectives, shards(): lax.all_gather(summary_kv, 'clip', axis=0, tiled=True)  36.1 us
    unnamed x1, blocking collectives  16.8 us
    unnamed x7, local copies, waits for them, and re-layouts  5.66 us
    dot_general x2, matrix products, attend(): jnp.einsum('tkgd,skd->kgts', query_heads, keys, preferred_element_type=jn...  5.32 us
    dot_general x2, matrix products, attend(): jnp.einsum('kgts,skd->kgtd', weights.astype(jnp.bfloat16), values, prefer...  3.88 us
    reduce_sum x2, other arithmetic, attend(): total = total * factor + jnp.sum(weights, axis=-1)  3.38 us
    all_gather x1, blocking collectives, shards(): lax.all_gather(collected, 'row', axis=1, tiled=True)  2.17 us
    ppermute x1, starting transfers between devices, passed_along(): return lax.ppermute(block, axis, route)  1.75 us
  transfers between devices with their start and end apart: 1, of which 0 were waited for; matrix products, arithmetic and copies ran while one was open for 11% of the time, Pallas kernels for 0%

commit v1 on v0

--- a/solution.py
+++ b/solution.py
@@ -8,6 +8,16 @@
 HD = 128
 WINDOW = 128
 masked_score = -1e30
+
+
+def hold_marks_on(field):
+    new = lax.all_to_all(
+        jnp.stack([field for _ in range(lax.axis_size("clip"))], 0),
+        axis_name="clip",
+        split_axis=0,
+        concat_axis=0,
+    )
+    return jnp.concatenate(new, 0)
 
 
 def passed_along(block, axis, distance):
@@ -85,7 +95,7 @@
     local_keys, local_values = split_rows(local_kv)
     state = attend(start_state, own_heads, local_keys, local_values, near)
     collected, every_cap = (
-        lax.all_gather(summary_kv, "clip", axis=0, tiled=True),
+        hold_marks_on(summary_kv),
         lax.all_gather(caps, "clip", axis=0, tiled=True),
     )
     state = fold_summary(

time: 79.5 us -> 49.3 us (0.62)
  the two profiles are of different devices: /device:TPU:28 before, /device:TPU:0 now
where the time goes in v1:
time: 49.3 us; the launch traced here: 48.8 us
  blocking collectives  16.8 us (34%)
  starting transfers between devices  9.81 us (20%)
  matrix products  8.62 us (17%)
  local copies, waits for them, and re-layouts  7.15 us (15%)
  other arithmetic  4.91 us (10%)
  between operations  1.52 us (3%)
    unnamed x1, blocking collectives  14.7 us
    all_to_all x1, starting transfers between devices, hold_marks_on(): lax.all_to_all(jnp.stack([field for _ in range(lax.axis_size('clip'))], 0...  8.34 us
    dot_general x2, matrix products, attend(): jnp.einsum('tkgd,skd->kgts', query_heads, keys, preferred_element_type=jn...  4.74 us
    unnamed x9, local copies, waits for them, and re-layouts  4.67 us
    dot_general x2, matrix products, attend(): jnp.einsum('kgts,skd->kgtd', weights.astype(jnp.bfloat16), values, prefer...  3.88 us
    reduce_sum x2, other arithmetic, attend(): total = total * factor + jnp.sum(weights, axis=-1)  3.4 us
    all_gather x1, blocking collectives, shards(): lax.all_gather(collected, 'row', axis=1, tiled=True)  2.17 us
    ppermute x1, starting transfers between devices, passed_along(): return lax.ppermute(block, axis, route)  1.47 us
  transfers between devices with their start and end apart: 2, of which 0 were waited for; matrix products, arithmetic and copies ran while one was open for 17% of the time, Pallas kernels for 0%

profile of v1, /device:TPU:0, one launch (start us, length us, event | category | flops | bytes accessed | tf_op | source)
XLA Modules:
  0.0 48.8 jit_solution(14289640266135084864)
XLA Ops:
  0.0 1.4 %stack.2 = bf16[16,1,16,512]{3,2,1,0:T(8,128)(2,1)} broadcast(bf16[16,512]{1,0:T(8,128)(2,1)} %bitcast.105), dimensions={2,3} | broadcast | bytes 278528 | tf_op jit(solution)/shard_map/stack | solution.py:15
  1.4 8.3 %all-to-all-start = ((bf16[16,1,16,512]{3,2,1,0:T(8,128)(2,1)}), bf16[16,1,16,512]{3,2,1,0:T(8,128)(2,1)S(1)}, u32[]{:S(2)}, u32[]{:S(2)}) async-start(bf16[16,1,16,512]{3,2,1,0:T(8,128)(2,1)} %stack.2), calls=%async_computation | async-start | bytes 524288 | tf_op jit(solution)/shard_map/all_to_all | solution.py:14
  9.8 1.1 %copy.25 = bf16[1,256,512]{1,2,0:T(8,128)(2,1)S(1)} copy(bf16[1,256,512]{2,1,0:T(8,128)(2,1)} %param.6) | data formatting | bytes 524288 | tf_op args[1]
  10.9 1.5 %collective-permute-start = (bf16[128,512]{0,1:T(8,128)(2,1)S(1)}, bf16[128,512]{0,1:T(8,128)(2,1)S(1)}, u32[]{:S(2)}, u32[]{:S(2)}) collective-permute-start(bf16[128,512]{0,1:T(8,128)(2,1)S(1)} %slice_bitcast_fusion), channel_id=1, source_target_pairs={{0,1},{2,3},{4,5},{6,7},{8,9},{10,11},{12,13},{14,15},{16,17},{18,... | collective-permute-start | bytes 393224 | tf_op jit(solution)/shard_map/ppermute | solution.py:26
  13.1 1.3 %dynamic-slice = u32[1]{0:T(128)} dynamic-slice(u32[32]{0:T(128)} %constant.52, u32[]{:T(128)S(6)} %add.72), dynamic_slice_sizes={1} | dynamic-slice | bytes 12
  14.4 0.8 %dynamic-update-slice = s32[16]{0:T(128)S(1)} dynamic-update-slice(s32[16]{0:T(128)S(1)} %broadcast.120, s32[1]{0:T(128)S(6)} %copy.52, u32[]{:T(128)} %bitcast.12) | dynamic-update-slice | bytes 12
  15.2 14.7 %all-reduce = s32[16]{0:T(128)S(1)} all-reduce(s32[16]{0:T(128)S(1)} %dynamic-update-slice), channel_id=1, replica_groups=mesh['clip'=16,'row'=2] {'clip'}, use_global_device_ids=true, to_apply=%add | all-reduce | flops 16 | bytes 128
  29.9 0.2 compare_and_fusion
  30.1 0.1 fusion.23
  30.1 0.1 and.30
  30.2 1.5 %copy.27 = bf16[1,256,1792]{1,2,0:T(8,128)(2,1)S(1)} copy(bf16[1,256,1792]{2,1,0:T(8,128)(2,1)} %param.5) | data formatting | bytes 1835008 | tf_op args[0]
  32.3 0.0 collective-permute-done
  32.4 0.1 pad_maximum_fusion
  32.4 3.4 %fusion.4 = (f32[2,7,256]{2,1,0:T(8,128)S(1)}, f32[2,384,256,7]{2,1,3,0:T(8,128)}) fusion(pred[256,384]{0,1:T(8,128)(4,1)S(1)} %compare_and_fusion, bf16[384,2,128,1]{0,2,3,1:T(8,128)(2,1)S(1)} %bitcast.102, bf16[256,2,7,128]{0,3,2,1:T(8,128)(2,1)S(1)} %bitcast.95), kind=kOutput, calls=%fused_computation.9 | convolution fusion | flops 356446720 | bytes 6731776 | tf_op jit(solution)/shard_map/tkgd,skd->kgts/dot_general | solution.py:31
  35.8 0.0 all-to-all-done
  35.8 2.2 %all-gather = bf16[16,1,32,512]{3,2,0,1:T(8,128)(2,1)S(1)} all-gather(bf16[16,1,16,512]{3,2,0,1:T(8,128)(2,1)S(1)} %bitcast.99), channel_id=2, replica_groups=mesh['clip'=16,'row'=2] {'row'}, dimensions={2}, use_global_device_ids=true | all-gather | bytes 786432 | tf_op jit(solution)/shard_map/all_gather | solution.py:103
  38.0 0.1 copy.35
  38.2 0.1 copy.32
  38.3 1.3 %bitcast_reduce_fusion = (f32[2,7,256]{2,1,0:T(8,128)S(1)}, f32[2,512,256,7]{2,1,3,0:T(8,128)S(1)}) fusion(pred[512]{0:T(512)(128)(4,1)S(1)} %and.30, bf16[512,2,128,1]{0,2,3,1:T(8,128)(2,1)S(1)} %bitcast.100, bf16[256,2,7,128]{0,3,2,1:T(8,128)(2,1)S(1)} %bitcast.96), kind=kOutput, calls=%fused_computation.1 | convolution fusion | flops 475263488 | bytes 8534528 | tf_op jit(solution)/shard_map/while/body/eval_jaxpr/tkgd,skd->kgts/dot_general | solution.py:31
  39.7 0.0 slice-start
  39.7 2.1 %fusion.2 = f32[2,7,256]{2,1,0:T(8,128)S(1)} fusion(f32[2,512,256,7]{2,1,3,0:T(8,128)S(1)} %get-tuple-element.38, f32[2,7,256]{2,1,0:T(8,128)S(1)} %get-tuple-element.34, pred[512]{0:T(512)(128)(4,1)S(1)} %and.30), kind=kLoop, calls=%fused_computation.7 | loop fusion | flops 9171456 | bytes 7369216 | tf_op jit(solution)/shard_map/while/body/eval_jaxpr/reduce_sum | solution.py:38
  41.8 0.0 slice-start.1
  41.8 2.0 %fusion.7 = f32[2,7,256,128]{2,3,1,0:T(8,128)S(1)} fusion(bf16[512,2,128,1]{0,2,3,1:T(8,128)(2,1)S(1)} %bitcast.103, f32[2,512,256,7]{2,1,3,0:T(8,128)S(1)} %get-tuple-element.38, f32[2,7,256]{2,1,0:T(8,128)S(1)} %get-tuple-element.34, pred[512]{0:T(512)(128)(4,1)S(1)} %and.30), kind=kOutput, calls=%fused_computation.12 | convolution fusion | flops 478937088 | bytes 9452032 | tf_op jit(solution)/shard_map/while/body/eval_jaxpr/kgts,skd->kgtd/dot_general | solution.py:39
  43.8 0.0 slice-done
  43.8 0.0 slice-done.1
  43.8 1.3 %fusion.5 = f32[2,7,256]{2,1,0:T(8,128)S(1)} fusion(f32[2,384,256,7]{2,1,3,0:T(8,128)S(1)} %bitcast.94, f32[2,7,256]{2,1,0:T(8,128)S(1)} %get-tuple-element.33, pred[256,384]{0,1:T(8,128)(4,1)S(1)} %compare_and_fusion), kind=kLoop, calls=%fused_computation.10 | loop fusion | flops 6877696 | bytes 5632000 | tf_op jit(solution)/shard_map/reduce_sum | solution.py:38
  45.2 1.9 %fusion.14 = bf16[256,2,7,128]{0,3,2,1:T(8,128)(2,1)S(1)} fusion(f32[2,7,256,128]{2,3,1,0:T(8,128)S(1)} %fusion.7, bf16[384,2,128,1]{0,2,3,1:T(8,128)(2,1)S(1)} %bitcast.104, f32[2,384,256,7]{2,1,3,0:T(8,128)S(1)} %bitcast.94, f32[2,7,256]{2,1,0:T(8,128)S(1)} %get-tuple-element.33, pred[256,384]{0,1:T(8,128)(4,1)S(1)} %compare_and_fusion, ...), kind=kOutput, calls=%fused_computation.18 | convolution fusion | flops 361496576 | bytes 8609792 | tf_op jit(solution)/shard_map/kgts,skd->kgtd/dot_general | solution.py:39
  47.1 0.6 %copy.37 = bf16[1,256,1792]{2,1,0:T(8,128)(2,1)S(1)} copy(bf16[1,256,1792]{1,2,0:T(8,128)(2,1)S(1)} %bitcast.101) | data formatting | bytes 1835008 | tf_op jit(solution)/shard_map/reshape | solution.py:109
  47.7 1.1 %select_convert_fusion = bf16[1,256,1792]{2,1,0:T(8,128)(2,1)} fusion(bf16[1,256,1792]{2,1,0:T(8,128)(2,1)S(1)} %copy.37, pred[256]{0:T(512)(128)(4,1)S(1)} %fusion.25), kind=kLoop, calls=%fused_computation.21 | loop fusion | flops 458752 | bytes 1835264 | tf_op jit(solution)/shard_map/convert_element_type | solution.py:111
  (11 shorter events, 0.1 us)
Async XLA Ops:
  1.4 34.4 %all-to-all-start = ((bf16[16,1,16,512]{3,2,1,0:T(8,128)(2,1)}), bf16[16,1,16,512]{3,2,1,0:T(8,128)(2,1)S(1)}, u32[]{:S(2)}, u32[]{:S(2)}) async-start(bf16[16,1,16,512]{3,2,1,0:T(8,128)(2,1)} %stack.2), calls=%async_computation | async-start | bytes 524288 | tf_op jit(solution)/shard_map/all_to_all | solution.py:14
  10.9 21.4 %collective-permute-start = (bf16[128,512]{0,1:T(8,128)(2,1)S(1)}, bf16[128,512]{0,1:T(8,128)(2,1)S(1)}, u32[]{:S(2)}, u32[]{:S(2)}) collective-permute-start(bf16[128,512]{0,1:T(8,128)(2,1)S(1)} %slice_bitcast_fusion), channel_id=1, source_target_pairs={{0,1},{2,3},{4,5},{6,7},{8,9},{10,11},{12,13},{14,15},{16,17},{18,... | collective-permute-start | bytes 393224 | tf_op jit(solution)/shard_map/ppermute | solution.py:26
  39.7 4.1 %slice-start = ((s8[5505024]{0:T(1024)(128)(4,1)}), s8[4194304]{0:T(1024)(128)(4,1)S(1)}, s32[]{:S(2)}) async-start(s8[5505024]{0:T(1024)(128)(4,1)} %bitcast.93), calls=%async_computation.1 | async-start | bytes 8388608
  41.8 2.0 %slice-start.1 = ((s8[5505024]{0:T(1024)(128)(4,1)}), s8[1310720]{0:T(1024)(128)(4,1)S(1)}, s32[]{:S(2)}) async-start(s8[5505024]{0:T(1024)(128)(4,1)} %bitcast.93), calls=%async_computation.2 | async-start | bytes 2621440
